TPU v7x, 32 devices: a whole 2x2x4 slice. The times are simulated.
32 devices in a mesh: dp: 16 (over z, y, core), expert: 2 (over x).
Axes of the slice: x: 2, y: 2, z: 4, core: 2. Of those that a mesh axis runs over, the one named last changes fastest.
Arguments:
- tokens: bfloat16 [4096, 2048], P(('dp', 'expert')), may hold values from -6 to 6
- cotangent: bfloat16 [4096, 2048], P(('dp', 'expert')), may hold values from -6 to 6
- expert_ids: int32 [4096, 8], P(('dp', 'expert')), may hold values from 0 to 127, as said below
- route_weights: float32 [4096, 8], P(('dp', 'expert')), may hold values from 0.1 to 1
- join_groups: int32 [16], replicated, may hold values from 0 to 1
- w_gate: bfloat16 [2048, 1024], P('dp', 'expert'), may hold values from -0.125 to 0.125
- w_up: bfloat16 [2048, 1024], P('dp', 'expert'), may hold values from -0.125 to 0.125
- w_down: bfloat16 [2048, 1024], P('dp', 'expert'), may hold values from -0.1875 to 0.1875
Outputs:
- mixed: bfloat16 [4096, 2048], P(('dp', 'expert'))
- grad_gate: bfloat16 [2048, 1024], P('dp', 'expert')
- grad_up: bfloat16 [2048, 1024], P('dp', 'expert')
- grad_down: bfloat16 [2048, 1024], P('dp', 'expert')
Inputs may be any that keep to these rules, and one draw needn't show every extreme that they name: `expert_ids`: each row names 8 different experts; the rows of one device name expert 0 at most 16 times, and the rows of some device exactly 16 times.
All inputs are finite; a program needn't handle non-finite values.
Results may differ from a plain program's by a relative error of at most 0.014.
Values may be sent and summed in bfloat16 or wider, within the bound.
A program may use at most 64 MiB of HBM per device.

v0:
```python
import jax
import jax.numpy as jnp
from jax import lax
from jax.sharding import PartitionSpec as P


def per_device(tokens, cotangent, expert_ids, route_weights, join_groups, w_gate, w_up, w_down):
    highest = lax.Precision.HIGHEST
    tok_count = tokens.shape[0]
    slot_count = tok_count // 8
    slice_width = w_gate.shape[1]
    chosen_mask = expert_ids == 0
    routed = jnp.any(chosen_mask, -1)
    weight = jnp.sum(jnp.where(chosen_mask, route_weights, 0.0), -1)
    places = jnp.cumsum(routed.astype(jnp.int32)) - 1
    slot_ids = jnp.arange(slot_count, dtype=jnp.int32)
    chooser = ((places[None, :] == slot_ids[:, None]) & routed[None, :]).astype(jnp.float32)
    chooser_half = chooser.astype(jnp.bfloat16)
    picked_local = jnp.dot(chooser_half, tokens, preferred_element_type=jnp.float32).astype(
        jnp.bfloat16
    )
    picked = lax.all_gather(picked_local, "expert", axis=0, tiled=True)
    gate_acts = jnp.dot(
        picked, lax.all_gather(w_gate, "dp", axis=0, tiled=True), preferred_element_type=jnp.float32
    )
    up_acts = jnp.dot(
        picked, lax.all_gather(w_up, "dp", axis=0, tiled=True), preferred_element_type=jnp.float32
    )
    hidden = (jax.nn.silu(gate_acts) * up_acts).astype(jnp.bfloat16)
    trans_dims = (((1,), (1,)), ((), ()))
    full_down = lax.all_gather(w_down, "dp", axis=0, tiled=True)
    partial_out = lax.dot_general(hidden, full_down, trans_dims, preferred_element_type=jnp.float32)
    out_rows = lax.psum_scatter(
        partial_out.astype(jnp.bfloat16), "expert", scatter_dimension=0, tiled=True
    ).astype(jnp.float32)
    placed = lax.dot_general(
        chooser,
        out_rows,
        (((0,), (0,)), ((), ())),
        precision=highest,
        preferred_element_type=jnp.float32,
    )
    mixed = (placed * weight[:, None]).astype(jnp.bfloat16)
    scaled = cotangent.astype(jnp.float32) * weight[:, None]
    dpicked_local = jnp.dot(
        chooser, scaled, precision=highest, preferred_element_type=jnp.float32
    ).astype(jnp.bfloat16)
    dpicked = lax.all_gather(dpicked_local, "expert", axis=0, tiled=True)
    hidden_grad = jnp.dot(dpicked, full_down, preferred_element_type=jnp.float32)
    sigma_gate = jax.nn.sigmoid(gate_acts)
    dgate = (hidden_grad * up_acts * sigma_gate * (1.0 + gate_acts * (1.0 - sigma_gate))).astype(
        jnp.bfloat16
    )
    dup = (hidden_grad * gate_acts * sigma_gate).astype(jnp.bfloat16)
    group_total = lax.axis_size("dp")
    mine = jnp.arange(group_total, dtype=jnp.int32) == lax.axis_index("dp")
    active = 1.0 - jnp.sum(jnp.where(mine, join_groups, 0)).astype(jnp.float32)
    col_dims = (((0,), (0,)), ((), ()))

    def term_of(left, right):
        return active * lax.dot_general(left, right, col_dims, preferred_element_type=jnp.float32)

    summed = lax.psum_scatter(
        jnp.concatenate(
            [term_of(picked, dgate), term_of(picked, dup), term_of(dpicked, hidden)], axis=1
        ),
        "dp",
        scatter_dimension=0,
        tiled=True,
    )
    grad_gate = summed[:, :slice_width]
    grad_up = summed[:, slice_width : 2 * slice_width]
    grad_down = summed[:, 2 * slice_width :]
    return (
        mixed,
        grad_gate.astype(jnp.bfloat16),
        grad_up.astype(jnp.bfloat16),
        grad_down.astype(jnp.bfloat16),
    )


def solution(mesh):
    in_specs = (
        P(("dp", "expert"), None),
        P(("dp", "expert"), None),
        P(("dp", "expert"), None),
        P(("dp", "expert"), None),
        P(),
        P("dp", "expert"),
        P("dp", "expert"),
        P("dp", "expert"),
    )
    out_specs = (P(("dp", "expert"), None), P("dp", "expert"), P("dp", "expert"), P("dp", "expert"))
    return jax.shard_map(
        per_device, mesh=mesh, in_specs=in_specs, out_specs=out_specs, check_vma=False
    )
```

profile of v0, /device:TPU:0, one launch (start us, length us, event | category | flops | bytes accessed | tf_op | source)
XLA Modules:
  0.0 300.2 jit_solution(16604740441010829208)
XLA Ops:
  8.0 0.7 all-gather.6.cloned.1.call-update
  8.7 0.7 all-gather.8.cloned.1.call-update
  9.5 1.3 fusion.15
  11.4 0.7 select_reduce_fusion
  12.5 1.6 convolution_convert_fusion.1
  14.2 5.9 %all_gather.19 = bf16[32,2048]{1,0:T(8,128)(2,1)S(1)} all-gather(bf16[16,2048]{1,0:T(8,128)(2,1)S(1)} %convolution_convert_fusion.1), channel_id=1, replica_groups=mesh['dp'=16,'expert'=2] {'expert'}, dimensions={0}, use_global_device_ids=true | all-gather | bytes 196608 | tf_op jit(solution)/shard_map/all_gather | solution.py:48
  20.2 4.9 %all_gather.15 = bf16[32,2048]{1,0:T(8,128)(2,1)S(1)} all-gather(bf16[16,2048]{1,0:T(8,128)(2,1)S(1)} %convolution_convert_fusion.2), channel_id=1, replica_groups=mesh['dp'=16,'expert'=2] {'expert'}, dimensions={0}, use_global_device_ids=true | all-gather | bytes 196608 | tf_op jit(solution)/shard_map/all_gather | solution.py:22
  25.1 29.2 %all-gather.4.cloned.1.call-done = bf16[2048,512]{1,0:T(8,128)(2,1)} async-done(((bf16[128,512]{1,0:T(8,128)(2,1)}), bf16[2048,512]{1,0:T(8,128)(2,1)}) %all-gather.4.cloned.1.call-update) | async-done | bytes 2097168 | tf_op jit(solution)/shard_map/all_gather | solution.py:24
  54.4 2.0 fusion.19
  56.4 40.3 %all-gather.6.cloned.1.call-done = bf16[2048,512]{1,0:T(8,128)(2,1)} async-done(((bf16[128,512]{1,0:T(8,128)(2,1)}), bf16[2048,512]{1,0:T(8,128)(2,1)}) %all-gather.6.cloned.1.call-update) | async-done | bytes 2097168 | tf_op jit(solution)/shard_map/all_gather | solution.py:27
  96.7 2.0 multiply_convert_fusion.2
  98.8 40.3 %all-gather.8.cloned.1.call-done = bf16[2048,512]{1,0:T(8,128)(2,1)} async-done(((bf16[128,512]{1,0:T(8,128)(2,1)}), bf16[2048,512]{1,0:T(8,128)(2,1)}) %all-gather.8.cloned.1.call-update) | async-done | bytes 2097168 | tf_op jit(solution)/shard_map/all_gather | solution.py:31
  139.1 3.1 %convolution_convert_fusion = bf16[32,2048]{1,0:T(8,128)(2,1)} fusion(bf16[32,512]{1,0:T(8,128)(2,1)S(1)} %get-tuple-element.17, bf16[2048,512]{1,0:T(8,128)(2,1)} %all-gather.8.cloned.1.call-done), kind=kOutput, calls=%fused_computation.6 | convolution fusion | flops 67174400 | bytes 2260992 | tf_op jit(solution)/shard_map/dot_general | solution.py:32
  142.3 0.7 convolution_multiply_fusion
  143.5 0.8 convolution_multiply_fusion.1
  144.3 0.8 convolution_multiply_fusion.2
  145.1 5.4 %pad_maximum_fusion = f32[2048,1536]{0,1:T(8,128)} fusion(f32[2048,512]{0,1:T(8,128)S(1)} %convolution_multiply_fusion, f32[2048,512]{0,1:T(8,128)S(1)} %convolution_multiply_fusion.1, f32[2048,512]{0,1:T(8,128)S(1)} %convolution_multiply_fusion.2), kind=kLoop, calls=%fused_computation | loop fusion | flops 6291456 | bytes 25165824 | tf_op jit(solution)/shard_map/concatenate | solution.py:64
  150.5 1.0 reduce-scatter.3.cloned.1.call-done
  151.5 2.0 fusion
  153.5 136.7 %reduce-scatter.5.cloned.1.call-done = f32[128,1536]{0,1:T(8,128)} async-done(((f32[2048,1536]{0,1:T(8,128)}), f32[128,1536]{0,1:T(8,128)}) %reduce-scatter.5.cloned.1.call-update) | async-done | bytes 786448 | tf_op jit(solution)/shard_map/reduce_scatter | solution.py:63
  290.2 1.2 convert.6
  291.4 0.8 copy.19
  292.2 0.8 copy.18
  292.9 0.8 copy.17
  (20 shorter events, 2.0 us)
Async XLA Ops:
  7.2 12.9 %copy-start = (bf16[128,2048]{1,0:T(8,128)(2,1)S(1)}, bf16[128,2048]{1,0:T(8,128)(2,1)}, u32[]{:S(2)}) copy-start(bf16[128,2048]{1,0:T(8,128)(2,1)} %param.8) | copy-start | bytes 1572868
  7.2 47.2 %all-gather.4.cloned.1.call-start = ((), (), s32[]{:S(2)}) async-start(), calls=%async_computation.2 | async-start | bytes 2228224 | tf_op jit(solution)/shard_map/all_gather | solution.py:24
  7.9 88.8 %all-gather.6.cloned.1.call-start = ((), (), s32[]{:S(2)}) async-start(), calls=%async_computation.3 | async-start | bytes 2228224 | tf_op jit(solution)/shard_map/all_gather | solution.py:27
  8.7 130.4 %all-gather.8.cloned.1.call-start = ((), (), s32[]{:S(2)}) async-start(), calls=%async_computation.4 | async-start | bytes 2228224 | tf_op jit(solution)/shard_map/all_gather | solution.py:31
  9.4 142.1 %reduce-scatter.3.cloned.1.call-start = ((), (), s32[]{:S(2)}) async-start(), calls=%async_computation.5 | async-start | bytes 196608 | tf_op jit(solution)/shard_map/reduce_scatter | solution.py:33
  139.1 4.0 %copy-start.1 = (bf16[2048,512]{1,0:T(8,128)(2,1)S(1)}, bf16[2048,512]{1,0:T(8,128)(2,1)}, u32[]{:S(2)}) copy-start(bf16[2048,512]{1,0:T(8,128)(2,1)} %all-gather.8.cloned.1.call-done) | copy-start | bytes 6291460
  142.3 147.9 %reduce-scatter.5.cloned.1.call-start = ((), (), s32[]{:S(2)}) async-start(), calls=%async_computation.6 | async-start | bytes 13369344 | tf_op jit(solution)/shard_map/reduce_scatter | solution.py:63
Sparse Core Ops, SparseCore 0:
  10.2 44.1 all-gather.3
  56.5 40.1 all-gather.5
  98.9 40.1 all-gather.7
  142.4 9.0 reduce-scatter.2
  155.4 134.7 reduce-scatter.4
where the time goes:
time: 301 us; the launch traced here: 300 us
  waiting for transfers between devices  250 us (83%)
  between operations  14.5 us (5%)
  matrix products  13.7 us (5%)
  blocking collectives  10.8 us (4%)
  other arithmetic  8.91 us (3%)
    reduce_scatter x1, waiting for transfers between devices, per_device(): lax.psum_scatter(jnp.concatenate([term_of(picked, dgate), term_of(picked,...  137 us
    all_gather x1, waiting for transfers between devices, per_device(): full_down = lax.all_gather(w_down, 'dp', axis=0, tiled=True)  40.3 us
    all_gather x1, waiting for transfers between devices, per_device(): lax.all_gather(w_up, 'dp', axis=0, tiled=True)  40.3 us
    all_gather x1, waiting for transfers between devices, per_device(): lax.all_gather(w_gate, 'dp', axis=0, tiled=True)  29.2 us
  transfers between devices with their start and end apart: 5, of which 5 were waited for; matrix products, arithmetic and copies ran while one was open for 6% of the time, Pallas kernels for 0%

commit v1 on v0

--- a/solution.py
+++ b/solution.py
@@ -20,9 +20,24 @@
         jnp.bfloat16
     )
     picked = lax.all_gather(picked_local, "expert", axis=0, tiled=True)
-    gate_acts = jnp.dot(
-        picked, lax.all_gather(w_gate, "dp", axis=0, tiled=True), preferred_element_type=jnp.float32
-    )
+
+    def bring_the_axis_part(slab_in):
+        res = lax.axis_index("dp")
+        right_arr = lax.axis_size("dp")
+        lower, parts_out, answer = (right_arr, res, slab_in.shape[0])
+        part_now = jnp.zeros(
+            (*slab_in.shape[:0], lower * answer, *slab_in.shape[1:]), slab_in.dtype
+        )
+        queue = [(u, (u + 1) % lower) for u in range(lower)]
+        r1 = slab_in
+        for idx in range(lower):
+            finding = (parts_out - idx) % lower
+            part_now = lax.dynamic_update_slice_in_dim(part_now, r1, finding * answer, axis=0)
+            if idx < lower - 1:
+                r1 = lax.ppermute(r1, axis_name="dp", perm=queue)
+        return part_now
+
+    gate_acts = jnp.dot(picked, bring_the_axis_part(w_gate), preferred_element_type=jnp.float32)
     up_acts = jnp.dot(
         picked, lax.all_gather(w_up, "dp", axis=0, tiled=True), preferred_element_type=jnp.float32
     )

time: 301 us -> 285 us (0.947)
  waiting for transfers between devices: 250 us -> 234 us
    ppermute x0 -> x15, waiting for transfers between devices: none -> 97.5 us  [bring_the_axis_part(): r1 = lax.ppermute(r1, axis_name='dp', perm=queue)]
    all_gather x1, waiting for transfers between devices: 40.3 us -> 0.01 us  [per_device(): lax.all_gather(w_up, 'dp', axis=0, tiled=True)]
    all_gather x1, waiting for transfers between devices: 40.3 us -> 0.03 us  [per_device(): full_down = lax.all_gather(w_down, 'dp', axis=0, tiled=True)]
    all_gather x1 -> x0, waiting for transfers between devices: 29.2 us -> none  [per_device(): lax.all_gather(w_gate, 'dp', axis=0, tiled=True)]
  transfers between devices with their start and end apart: 5 -> 19, of which waited for: 5 -> 16; matrix products, arithmetic and copies ran while one was open for 6% -> 6% of each run, Pallas kernels for 0% -> 0%
where the time goes in v1:
time: 285 us; the launch traced here: 284 us
  waiting for transfers between devices  234 us (82%)
  between operations  14.7 us (5%)
  matrix products  12 us (4%)
  blocking collectives  10.2 us (4%)
  other arithmetic  8.93 us (3%)
  local copies, waits for them, and re-layouts  3.62 us (1%)
    reduce_scatter x1, waiting for transfers between devices, per_device(): lax.psum_scatter(jnp.concatenate([term_of(picked, dgate), term_of(picked,...  135 us
    ppermute x15, waiting for transfers between devices, bring_the_axis_part(): r1 = lax.ppermute(r1, axis_name='dp', perm=queue)  97.5 us
  transfers between devices with their start and end apart: 19, of which 16 were waited for; matrix products, arithmetic and copies ran while one was open for 6% of the time, Pallas kernels for 0%

profile of v1, /device:TPU:0, one launch (start us, length us, event | category | flops | bytes accessed | tf_op | source)
XLA Modules:
  0.0 284.5 jit_solution(8584436386957484149)
XLA Ops:
  9.3 7.8 %collective-permute-done = bf16[128,512]{1,0:T(8,128)(2,1)S(1)} collective-permute-done((bf16[128,512]{1,0:T(8,128)(2,1)}, bf16[128,512]{1,0:T(8,128)(2,1)S(1)}, u32[]{:S(2)}, u32[]{:S(2)}) %collective-permute-start) | collective-permute-done | bytes 131104 | tf_op jit(solution)/shard_map/ppermute | solution.py:37
  17.1 7.2 %collective-permute-done.1 = bf16[128,512]{1,0:T(8,128)(2,1)S(1)} collective-permute-done((bf16[128,512]{1,0:T(8,128)(2,1)S(1)}, bf16[128,512]{1,0:T(8,128)(2,1)S(1)}, u32[]{:S(2)}, u32[]{:S(2)}) %collective-permute-start.1) | collective-permute-done | bytes 131104 | tf_op jit(solution)/shard_map/ppermute | solution.py:37
  25.0 7.8 %collective-permute-done.2 = bf16[128,512]{1,0:T(8,128)(2,1)S(1)} collective-permute-done((bf16[128,512]{1,0:T(8,128)(2,1)S(1)}, bf16[128,512]{1,0:T(8,128)(2,1)S(1)}, u32[]{:S(2)}, u32[]{:S(2)}) %collective-permute-start.2) | collective-permute-done | bytes 131104 | tf_op jit(solution)/shard_map/ppermute | solution.py:37
  33.2 6.7 %collective-permute-done.3 = bf16[128,512]{1,0:T(8,128)(2,1)S(1)} collective-permute-done((bf16[128,512]{1,0:T(8,128)(2,1)S(1)}, bf16[128,512]{1,0:T(8,128)(2,1)S(1)}, u32[]{:S(2)}, u32[]{:S(2)}) %collective-permute-start.3) | collective-permute-done | bytes 131104 | tf_op jit(solution)/shard_map/ppermute | solution.py:37
  39.9 1.6 convolution_convert_fusion.1
  41.5 7.5 %collective-permute-done.4 = bf16[128,512]{1,0:T(8,128)(2,1)S(1)} collective-permute-done((bf16[128,512]{1,0:T(8,128)(2,1)S(1)}, bf16[128,512]{1,0:T(8,128)(2,1)S(1)}, u32[]{:S(2)}, u32[]{:S(2)}) %collective-permute-start.4) | collective-permute-done | bytes 131104 | tf_op jit(solution)/shard_map/ppermute | solution.py:37
  49.2 7.0 %collective-permute-done.5 = bf16[128,512]{1,0:T(8,128)(2,1)S(1)} collective-permute-done((bf16[128,512]{1,0:T(8,128)(2,1)S(1)}, bf16[128,512]{1,0:T(8,128)(2,1)S(1)}, u32[]{:S(2)}, u32[]{:S(2)}) %collective-permute-start.5) | collective-permute-done | bytes 131104 | tf_op jit(solution)/shard_map/ppermute | solution.py:37
  56.2 5.2 %all_gather.15 = bf16[32,2048]{1,0:T(8,128)(2,1)S(1)} all-gather(bf16[16,2048]{1,0:T(8,128)(2,1)S(1)} %convolution_convert_fusion.1), channel_id=1, replica_groups=mesh['dp'=16,'expert'=2] {'expert'}, dimensions={0}, use_global_device_ids=true | all-gather | bytes 196608 | tf_op jit(solution)/shard_map/all_gather | solution.py:63
  61.4 1.3 fusion.15
  63.3 4.9 %all_gather.12 = bf16[32,2048]{1,0:T(8,128)(2,1)S(1)} all-gather(bf16[16,2048]{1,0:T(8,128)(2,1)S(1)} %convolution_convert_fusion.2), channel_id=1, replica_groups=mesh['dp'=16,'expert'=2] {'expert'}, dimensions={0}, use_global_device_ids=true | all-gather | bytes 196608 | tf_op jit(solution)/shard_map/all_gather | solution.py:22
  69.1 1.4 collective-permute-done.7
  70.5 7.4 %collective-permute-done.8 = bf16[128,512]{1,0:T(8,128)(2,1)S(1)} collective-permute-done((bf16[128,512]{1,0:T(8,128)(2,1)S(1)}, bf16[128,512]{1,0:T(8,128)(2,1)S(1)}, u32[]{:S(2)}, u32[]{:S(2)}) %collective-permute-start.8) | collective-permute-done | bytes 131104 | tf_op jit(solution)/shard_map/ppermute | solution.py:37
  78.0 7.0 %collective-permute-done.9 = bf16[128,512]{1,0:T(8,128)(2,1)S(1)} collective-permute-done((bf16[128,512]{1,0:T(8,128)(2,1)S(1)}, bf16[128,512]{1,0:T(8,128)(2,1)S(1)}, u32[]{:S(2)}, u32[]{:S(2)}) %collective-permute-start.9) | collective-permute-done | bytes 131104 | tf_op jit(solution)/shard_map/ppermute | solution.py:37
  85.1 8.6 %collective-permute-done.10 = bf16[128,512]{1,0:T(8,128)(2,1)S(1)} collective-permute-done((bf16[128,512]{1,0:T(8,128)(2,1)S(1)}, bf16[128,512]{1,0:T(8,128)(2,1)S(1)}, u32[]{:S(2)}, u32[]{:S(2)}) %collective-permute-start.10) | collective-permute-done | bytes 131104 | tf_op jit(solution)/shard_map/ppermute | solution.py:37
  93.7 7.4 %collective-permute-done.11 = bf16[128,512]{1,0:T(8,128)(2,1)S(1)} collective-permute-done((bf16[128,512]{1,0:T(8,128)(2,1)S(1)}, bf16[128,512]{1,0:T(8,128)(2,1)S(1)}, u32[]{:S(2)}, u32[]{:S(2)}) %collective-permute-start.11) | collective-permute-done | bytes 131104 | tf_op jit(solution)/shard_map/ppermute | solution.py:37
  101.2 7.0 %collective-permute-done.12 = bf16[128,512]{1,0:T(8,128)(2,1)S(1)} collective-permute-done((bf16[128,512]{1,0:T(8,128)(2,1)S(1)}, bf16[128,512]{1,0:T(8,128)(2,1)S(1)}, u32[]{:S(2)}, u32[]{:S(2)}) %collective-permute-start.12) | collective-permute-done | bytes 131104 | tf_op jit(solution)/shard_map/ppermute | solution.py:37
  108.2 7.0 %collective-permute-done.13 = bf16[128,512]{1,0:T(8,128)(2,1)S(1)} collective-permute-done((bf16[128,512]{1,0:T(8,128)(2,1)S(1)}, bf16[128,512]{1,0:T(8,128)(2,1)S(1)}, u32[]{:S(2)}, u32[]{:S(2)}) %collective-permute-start.13) | collective-permute-done | bytes 131104 | tf_op jit(solution)/shard_map/ppermute | solution.py:37
  115.3 7.0 %collective-permute-done.14 = bf16[128,512]{1,0:T(8,128)(2,1)S(1)} collective-permute-done((bf16[128,512]{1,0:T(8,128)(2,1)S(1)}, bf16[128,512]{1,0:T(8,128)(2,1)S(1)}, u32[]{:S(2)}, u32[]{:S(2)}) %collective-permute-start.14) | collective-permute-done | bytes 131104 | tf_op jit(solution)/shard_map/ppermute | solution.py:37
  122.9 2.0 multiply_convert_fusion.2
  124.9 3.0 %convolution_convert_fusion = bf16[32,2048]{1,0:T(8,128)(2,1)} fusion(bf16[32,512]{1,0:T(8,128)(2,1)S(1)} %get-tuple-element.17, bf16[2048,512]{1,0:T(8,128)(2,1)} %all-gather.5.cloned.1.call-done), kind=kOutput, calls=%fused_computation.6 | convolution fusion | flops 67174400 | bytes 2260992 | tf_op jit(solution)/shard_map/dot_general | solution.py:47
  131.5 5.4 %pad_maximum_fusion = f32[2048,1536]{0,1:T(8,128)} fusion(f32[2048,512]{0,1:T(8,128)S(1)} %convolution_multiply_fusion, f32[2048,512]{0,1:T(8,128)S(1)} %convolution_multiply_fusion.1, f32[2048,512]{0,1:T(8,128)S(1)} %convolution_multiply_fusion.2), kind=kLoop, calls=%fused_computation | loop fusion | flops 6291456 | bytes 25165824 | tf_op jit(solution)/shard_map/concatenate | solution.py:79
  137.0 2.0 fusion
  139.0 135.4 %reduce-scatter.5.cloned.1.call-done = f32[128,1536]{0,1:T(8,128)} async-done(((f32[2048,1536]{0,1:T(8,128)}), f32[128,1536]{0,1:T(8,128)}) %reduce-scatter.5.cloned.1.call-update) | async-done | bytes 786448 | tf_op jit(solution)/shard_map/reduce_scatter | solution.py:78
  274.4 1.2 convert.6
  (66 shorter events, 10.8 us)
Async XLA Ops:
  7.2 41.9 %copy-start = (bf16[128,2048]{1,0:T(8,128)(2,1)S(1)}, bf16[128,2048]{1,0:T(8,128)(2,1)}, u32[]{:S(2)}) copy-start(bf16[128,2048]{1,0:T(8,128)(2,1)} %param.8) | copy-start | bytes 1572868
  7.2 115.7 %all-gather.3.cloned.1.call-start = ((), (), s32[]{:S(2)}) async-start(), calls=%async_computation.2 | async-start | bytes 2228224 | tf_op jit(solution)/shard_map/all_gather | solution.py:42
  7.9 117.0 %all-gather.5.cloned.1.call-start = ((), (), s32[]{:S(2)}) async-start(), calls=%async_computation.3 | async-start | bytes 2228224 | tf_op jit(solution)/shard_map/all_gather | solution.py:46
  8.7 128.4 %reduce-scatter.3.cloned.1.call-start = ((), (), s32[]{:S(2)}) async-start(), calls=%async_computation.4 | async-start | bytes 196608 | tf_op jit(solution)/shard_map/reduce_scatter | solution.py:48
  8.7 8.4 %collective-permute-start = (bf16[128,512]{1,0:T(8,128)(2,1)}, bf16[128,512]{1,0:T(8,128)(2,1)S(1)}, u32[]{:S(2)}, u32[]{:S(2)}) collective-permute-start(bf16[128,512]{1,0:T(8,128)(2,1)} %param.13), channel_id=1, source_target_pairs={{0,2},{2,4},{4,6},{6,8},{8,10},{10,12},{12,14},{14,16},{16,18},{18... | collective-permute-start | bytes 393224 | tf_op jit(solution)/shard_map/ppermute | solution.py:37
  17.1 7.2 %collective-permute-start.1 = (bf16[128,512]{1,0:T(8,128)(2,1)S(1)}, bf16[128,512]{1,0:T(8,128)(2,1)S(1)}, u32[]{:S(2)}, u32[]{:S(2)}) collective-permute-start(bf16[128,512]{1,0:T(8,128)(2,1)S(1)} %collective-permute-done), channel_id=1, source_target_pairs={{0,2},{2,4},{4,6},{6,8},{8,10},{10,12},{12,14},{14,16},{16,18},{18... | collective-permute-start | bytes 393224 | tf_op jit(solution)/shard_map/ppermute | solution.py:37
  24.3 8.6 %collective-permute-start.2 = (bf16[128,512]{1,0:T(8,128)(2,1)S(1)}, bf16[128,512]{1,0:T(8,128)(2,1)S(1)}, u32[]{:S(2)}, u32[]{:S(2)}) collective-permute-start(bf16[128,512]{1,0:T(8,128)(2,1)S(1)} %collective-permute-done.1), channel_id=1, source_target_pairs={{0,2},{2,4},{4,6},{6,8},{8,10},{10,12},{12,14},{14,16},{16,18},{18... | collective-permute-start | bytes 393224 | tf_op jit(solution)/shard_map/ppermute | solution.py:37
  32.8 7.1 %collective-permute-start.3 = (bf16[128,512]{1,0:T(8,128)(2,1)S(1)}, bf16[128,512]{1,0:T(8,128)(2,1)S(1)}, u32[]{:S(2)}, u32[]{:S(2)}) collective-permute-start(bf16[128,512]{1,0:T(8,128)(2,1)S(1)} %collective-permute-done.2), channel_id=1, source_target_pairs={{0,2},{2,4},{4,6},{6,8},{8,10},{10,12},{12,14},{14,16},{16,18},{18... | collective-permute-start | bytes 393224 | tf_op jit(solution)/shard_map/ppermute | solution.py:37
  33.2 35.8 %copy-start.2 = (bf16[128,512]{1,0:T(8,128)(2,1)S(1)}, bf16[128,512]{1,0:T(8,128)(2,1)}, u32[]{:S(2)}) copy-start(bf16[128,512]{1,0:T(8,128)(2,1)} %param.13) | copy-start | bytes 393220
  39.9 9.1 %collective-permute-start.4 = (bf16[128,512]{1,0:T(8,128)(2,1)S(1)}, bf16[128,512]{1,0:T(8,128)(2,1)S(1)}, u32[]{:S(2)}, u32[]{:S(2)}) collective-permute-start(bf16[128,512]{1,0:T(8,128)(2,1)S(1)} %collective-permute-done.3), channel_id=1, source_target_pairs={{0,2},{2,4},{4,6},{6,8},{8,10},{10,12},{12,14},{14,16},{16,18},{18... | collective-permute-start | bytes 393224 | tf_op jit(solution)/shard_map/ppermute | solution.py:37
  49.0 7.1 %collective-permute-start.5 = (bf16[128,512]{1,0:T(8,128)(2,1)S(1)}, bf16[128,512]{1,0:T(8,128)(2,1)S(1)}, u32[]{:S(2)}, u32[]{:S(2)}) collective-permute-start(bf16[128,512]{1,0:T(8,128)(2,1)S(1)} %collective-permute-done.4), channel_id=1, source_target_pairs={{0,2},{2,4},{4,6},{6,8},{8,10},{10,12},{12,14},{14,16},{16,18},{18... | collective-permute-start | bytes 393224 | tf_op jit(solution)/shard_map/ppermute | solution.py:37
  56.2 7.1 %collective-permute-start.6 = (bf16[128,512]{1,0:T(8,128)(2,1)S(1)}, bf16[128,512]{1,0:T(8,128)(2,1)S(1)}, u32[]{:S(2)}, u32[]{:S(2)}) collective-permute-start(bf16[128,512]{1,0:T(8,128)(2,1)S(1)} %collective-permute-done.5), channel_id=1, source_target_pairs={{0,2},{2,4},{4,6},{6,8},{8,10},{10,12},{12,14},{14,16},{16,18},{18... | collective-permute-start | bytes 393224 | tf_op jit(solution)/shard_map/ppermute | solution.py:37
  63.3 7.2 %collective-permute-start.7 = (bf16[128,512]{1,0:T(8,128)(2,1)S(1)}, bf16[128,512]{1,0:T(8,128)(2,1)S(1)}, u32[]{:S(2)}, u32[]{:S(2)}) collective-permute-start(bf16[128,512]{1,0:T(8,128)(2,1)S(1)} %collective-permute-done.6), channel_id=1, source_target_pairs={{0,2},{2,4},{4,6},{6,8},{8,10},{10,12},{12,14},{14,16},{16,18},{18... | collective-permute-start | bytes 393224 | tf_op jit(solution)/shard_map/ppermute | solution.py:37
  70.5 7.5 %collective-permute-start.8 = (bf16[128,512]{1,0:T(8,128)(2,1)S(1)}, bf16[128,512]{1,0:T(8,128)(2,1)S(1)}, u32[]{:S(2)}, u32[]{:S(2)}) collective-permute-start(bf16[128,512]{1,0:T(8,128)(2,1)S(1)} %collective-permute-done.7), channel_id=1, source_target_pairs={{0,2},{2,4},{4,6},{6,8},{8,10},{10,12},{12,14},{14,16},{16,18},{18... | collective-permute-start | bytes 393224 | tf_op jit(solution)/shard_map/ppermute | solution.py:37
  78.0 7.1 %collective-permute-start.9 = (bf16[128,512]{1,0:T(8,128)(2,1)S(1)}, bf16[128,512]{1,0:T(8,128)(2,1)S(1)}, u32[]{:S(2)}, u32[]{:S(2)}) collective-permute-start(bf16[128,512]{1,0:T(8,128)(2,1)S(1)} %collective-permute-done.8), channel_id=1, source_target_pairs={{0,2},{2,4},{4,6},{6,8},{8,10},{10,12},{12,14},{14,16},{16,18},{18... | collective-permute-start | bytes 393224 | tf_op jit(solution)/shard_map/ppermute | solution.py:37
  85.0 8.6 %collective-permute-start.10 = (bf16[128,512]{1,0:T(8,128)(2,1)S(1)}, bf16[128,512]{1,0:T(8,128)(2,1)S(1)}, u32[]{:S(2)}, u32[]{:S(2)}) collective-permute-start(bf16[128,512]{1,0:T(8,128)(2,1)S(1)} %collective-permute-done.9), channel_id=1, source_target_pairs={{0,2},{2,4},{4,6},{6,8},{8,10},{10,12},{12,14},{14,16},{16,18},{18... | collective-permute-start | bytes 393224 | tf_op jit(solution)/shard_map/ppermute | solution.py:37
  93.7 7.4 %collective-permute-start.11 = (bf16[128,512]{1,0:T(8,128)(2,1)S(1)}, bf16[128,512]{1,0:T(8,128)(2,1)S(1)}, u32[]{:S(2)}, u32[]{:S(2)}) collective-permute-start(bf16[128,512]{1,0:T(8,128)(2,1)S(1)} %collective-permute-done.10), channel_id=1, source_target_pairs={{0,2},{2,4},{4,6},{6,8},{8,10},{10,12},{12,14},{14,16},{16,18},{18... | collective-permute-start | bytes 393224 | tf_op jit(solution)/shard_map/ppermute | solution.py:37
  101.1 7.1 %collective-permute-start.12 = (bf16[128,512]{1,0:T(8,128)(2,1)S(1)}, bf16[128,512]{1,0:T(8,128)(2,1)S(1)}, u32[]{:S(2)}, u32[]{:S(2)}) collective-permute-start(bf16[128,512]{1,0:T(8,128)(2,1)S(1)} %collective-permute-done.11), channel_id=1, source_target_pairs={{0,2},{2,4},{4,6},{6,8},{8,10},{10,12},{12,14},{14,16},{16,18},{18... | collective-permute-start | bytes 393224 | tf_op jit(solution)/shard_map/ppermute | solution.py:37
  108.2 7.1 %collective-permute-start.13 = (bf16[128,512]{1,0:T(8,128)(2,1)S(1)}, bf16[128,512]{1,0:T(8,128)(2,1)S(1)}, u32[]{:S(2)}, u32[]{:S(2)}) collective-permute-start(bf16[128,512]{1,0:T(8,128)(2,1)S(1)} %collective-permute-done.12), channel_id=1, source_target_pairs={{0,2},{2,4},{4,6},{6,8},{8,10},{10,12},{12,14},{14,16},{16,18},{18... | collective-permute-start | bytes 393224 | tf_op jit(solution)/shard_map/ppermute | solution.py:37
  115.3 7.1 %collective-permute-start.14 = (bf16[128,512]{1,0:T(8,128)(2,1)S(1)}, bf16[128,512]{1,0:T(8,128)(2,1)S(1)}, u32[]{:S(2)}, u32[]{:S(2)}) collective-permute-start(bf16[128,512]{1,0:T(8,128)(2,1)S(1)} %collective-permute-done.13), channel_id=1, source_target_pairs={{0,2},{2,4},{4,6},{6,8},{8,10},{10,12},{12,14},{14,16},{16,18},{18... | collective-permute-start | bytes 393224 | tf_op jit(solution)/shard_map/ppermute | solution.py:37
  127.9 1.6 copy-start.1
  127.9 146.5 %reduce-scatter.5.cloned.1.call-start = ((), (), s32[]{:S(2)}) async-start(), calls=%async_computation.5 | async-start | bytes 13369344 | tf_op jit(solution)/shard_map/reduce_scatter | solution.py:78
Sparse Core Ops, SparseCore 0:
  10.2 46.2 all-gather.2
  58.6 42.6 all-gather.4
  128.1 7.5 reduce-scatter.2
  139.6 134.7 reduce-scatter.4
